TPU v7x, 128 devices: a whole 4x4x4 slice. The times are simulated.
128 devices in a mesh: shot: 8 (over x, z_hi), dom: 16 (over z_lo, y, core).
Axes of the slice: x: 4, y: 4, z: 4 (z_hi: 2, z_lo: 2; z = z_hi * 2 + z_lo), core: 2. Of those that a mesh axis runs over, the one named last changes fastest.
Arguments:
- velocity: float32 [512, 32, 128], P('dom'), may hold values from 1.5 to 3
- noise_field: float32 [512, 32, 128], P('dom'), may hold values from -6 to 6
- step_size: float32 [1], replicated, may hold values from 0.05 to 0.5
- field_prev: float32 [16, 512, 32, 128], P('shot', 'dom'), may hold values from -6 to 6
- field_now: float32 [16, 512, 32, 128], P('shot', 'dom'), may hold values from -6 to 6
- adjoint_next: float32 [16, 512, 32, 128], P('shot', 'dom'), may hold values from -6 to 6
- adjoint_now: float32 [16, 512, 32, 128], P('shot', 'dom'), may hold values from -6 to 6
- wavelet: float32 [16, 4], P('shot'), may hold values from -8 to 8
- source_cells: int32 [16, 8], P('shot'), may hold values from 0 to 2097151
- source_signs: int32 [16, 8], P('shot'), may hold values from 0 to 1
- record_cells: int32 [16, 256], P('shot'), may hold values from 0 to 2097151
- observed: float32 [16, 4, 256], P('shot'), may hold values from -6 to 6
Outputs:
- new_velocity: float32 [512, 32, 128], P('dom', None, 'shot')
Inputs may be any that keep to these rules, and one draw needn't show every extreme that they name: `source_signs`: 0 stands for a negative sign, 1 for a positive one. `source_cells`: cells flattened as x 32 * 128 + z * 128 + y. `record_cells`: cells flattened as x 32 * 128 + z * 128 + y.
All inputs are finite; a program needn't handle non-finite values.
Results may differ from a plain program's by a relative error of at most 0.00009.
Values sent between devices are 32-bit elements; how exact they have to be, the bound alone decides.
No kernel may reach another device: no remote copies, remote signals or barrier semaphores. Data moves between devices by JAX's collectives and lax.ppermute only.
A program may use at most 128 MiB of HBM per device.

v0:
```python
import math
import jax
import jax.numpy as jnp
from jax import lax
from jax.sharding import PartitionSpec as P

STEPS = 4
COEFFS = (-205.0 / 72.0, 8.0 / 5.0, -1.0 / 5.0, 8.0 / 315.0, -1.0 / 560.0)
COURANT = 0.02


def extended(block, sides, width):
    for axis, dim in sides:
        count = lax.axis_size(axis)
        forward = [(i, i + 1) for i in range(count - 1)]
        backward = [(target, source) for source, target in forward]
        low = lax.ppermute(
            lax.slice_in_dim(block, block.shape[dim] - width, None, axis=dim), axis, forward
        )
        high = lax.ppermute(lax.slice_in_dim(block, 0, width, axis=dim), axis, backward)
        block = jnp.concatenate([low, block, high], axis=dim)
    return block


def stencil(padded):
    margin = 4
    rank = padded.ndim
    lengths = [padded.shape[rank - 3 + place] - 2 * margin for place in range(3)]

    def window(offsets):
        sliced = padded
        for place in range(3):
            begin = margin + offsets[place]
            sliced = lax.slice_in_dim(sliced, begin, begin + lengths[place], axis=rank - 3 + place)
        return sliced

    summed = 3.0 * COEFFS[0] * window((0, 0, 0))
    for distance in range(1, 5):
        beside_all = window((distance, 0, 0)) + window((-distance, 0, 0))
        beside_all = beside_all + window((0, distance, 0)) + window((0, -distance, 0))
        beside_all = beside_all + window((0, 0, distance)) + window((0, 0, -distance))
        summed = summed + COEFFS[distance] * beside_all
    return summed


def cosine_basis(length):
    wave_index = jnp.arange(length, dtype=jnp.int32)[:, None]
    position = jnp.arange(length, dtype=jnp.int32)[None, :]
    phase = wave_index * (2 * position + 1) % (4 * length)
    angle = math.pi / (2.0 * length) * phase.astype(jnp.float32)
    factor = jnp.where(wave_index == 0, math.sqrt(1.0 / length), math.sqrt(2.0 / length)).astype(
        jnp.float32
    )
    return factor * jnp.cos(angle)


def prior_gain(length, cutoff):
    scaled = jnp.arange(length, dtype=jnp.float32) / float(cutoff)
    return 1.0 / jnp.sqrt(1.0 + scaled)


def precondition(gradient, noise_cols, rate):
    length = gradient.shape[0]
    basis = cosine_basis(length)
    spectrum = prior_gain(length, length // 32)[:, None]
    highest = lax.Precision.HIGHEST
    grad_hat = jnp.dot(basis, gradient.reshape(length, -1), precision=highest)
    noise_hat = jnp.dot(basis, noise_cols.reshape(length, -1), precision=highest)
    weights = spectrum * (-0.5 * rate * spectrum * grad_hat + jnp.sqrt(rate) * noise_hat)
    update = lax.dot_general(basis, weights, (((0,), (0,)), ((), ())), precision=highest)
    return update.reshape(gradient.shape)


def widen(padded):
    return jnp.pad(padded, ((0, 0), (0, 0), (4, 4), (4, 4)))


def body(
    velocity,
    noise_field,
    step_size,
    field_prev,
    field_now,
    adjoint_next,
    adjoint_now,
    wavelet,
    source_cells,
    source_signs,
    record_cells,
    observed,
):
    speed_sq = COURANT * velocity * velocity
    shots_here = field_now.shape[0]
    slab_rows = velocity.shape[0]
    plane_cells = velocity.shape[1] * velocity.shape[2]
    slab_cells = slab_rows * plane_cells
    first_row = lax.axis_index("dom") * slab_rows
    offset = first_row * plane_cells
    row_ids = jnp.arange(shots_here, dtype=jnp.int32)[:, None]
    source_local = source_cells - offset
    source_inside = (source_local >= 0) & (source_local < slab_cells)
    source_target = jnp.where(source_inside, source_local, slab_cells)
    record_local = record_cells - offset
    record_inside = (record_local >= 0) & (record_local < slab_cells)
    record_target = jnp.where(record_inside, record_local, slab_cells)
    record_clip = jnp.clip(record_local, 0, slab_cells - 1)
    amplitude = (2 * source_signs - 1).astype(jnp.float32)

    def place(field, target, values):
        flat = field.reshape(shots_here, -1)
        rows_full = jnp.broadcast_to(row_ids, target.shape)
        return flat.at[rows_full, target].add(values, mode="drop").reshape(field.shape)

    summed = jnp.zeros(field_now.shape, jnp.float32)
    prior, current = (field_prev, field_now)
    laplacians = []
    samples = []
    for moment in range(STEPS):
        padded = extended(current, (("dom", 1),), 4)
        spread = stencil(widen(padded))
        laplacians.append(spread)
        advanced = 2.0 * current - prior + speed_sq * spread
        advanced = place(advanced, source_target, amplitude * wavelet[:, moment][:, None])
        samples.append(jnp.take_along_axis(advanced.reshape(shots_here, -1), record_clip, axis=1))
        prior, current = (current, advanced)
    adj_later, adj_current = (adjoint_next, adjoint_now)
    for moment in range(STEPS, 0, -1):
        misfit = samples[moment - 1] - observed[:, moment - 1, :]
        padded = extended(adj_current, (("dom", 1),), 4)
        spread = stencil(widen(padded))
        earlier = 2.0 * adj_current - adj_later + speed_sq * spread
        earlier = place(earlier, record_target, misfit)
        adj_later, adj_current = (adj_current, earlier)
        summed = summed + adj_current * laplacians[moment - 1]
    partial_value = 2.0 * COURANT * velocity * jnp.sum(summed, axis=0)
    rate = step_size[0]
    shot_rows = velocity.shape[2] // lax.axis_size("shot")
    start = lax.axis_index("shot") * shot_rows
    total = lax.psum(partial_value, "shot")
    grad_cols, noise_cols = (
        lax.all_to_all(total, "dom", split_axis=2, concat_axis=0, tiled=True),
        lax.all_to_all(noise_field, "dom", split_axis=2, concat_axis=0, tiled=True),
    )
    update = precondition(grad_cols, noise_cols, rate)
    returned = lax.all_to_all(update, "dom", split_axis=0, concat_axis=2, tiled=True)
    result = lax.dynamic_slice_in_dim(velocity + returned, start, shot_rows, 2)
    return result


def solution(mesh):
    placed = (
        P("dom", None, None),
        P("dom", None, None),
        P(),
        P("shot", "dom", None, None),
        P("shot", "dom", None, None),
        P("shot", "dom", None, None),
        P("shot", "dom", None, None),
        P("shot", None),
        P("shot", None),
        P("shot", None),
        P("shot", None),
        P("shot", None, None),
    )
    return jax.shard_map(
        body, mesh=mesh, in_specs=placed, out_specs=P("dom", None, "shot"), check_vma=False
    )
```

profile of v0, /device:TPU:1, one launch (start us, length us, event | category | flops | bytes accessed | tf_op | source)
XLA Modules:
  0.0 571.0 jit_solution(9023833268099805198)
XLA Ops:
  7.5 4.6 collective-permute-start.3
  15.7 3.6 collective-permute-start.1
  37.4 8.3 %multiply_add_fusion.3 = (f32[2,32,32,128]{3,2,1,0:T(8,128)}, f32[2,32,32,128]{3,2,1,0:T(8,128)}) fusion(f32[2,32,32,128]{3,2,1,0:T(8,128)} %param.17, f32[2,32,32,128]{3,2,1,0:T(8,128)} %param.18, f32[32,32,128]{2,1,0:T(8,128)} %multiply_multiply_fusion, f32[2,40,40,136]{3,2,1,0:T(8,128)S(1)} %select_maximum_fusion.12, f32[2,36,32,128]{3,2,1,0:T(8,128)} %copy-done.23, ...), kind=kLoop, calls=%fused_computation.293 | loop fusion | flops 8650752 | bytes 29884416 | tf_op jit(solution)/shard_map/add | solution.py:122
  49.7 3.9 collective-permute-start.5
  53.6 2.4 collective-permute-start.4
  56.1 2.5 select_maximum_fusion.14
  62.9 2.6 select_maximum_fusion.10
  66.2 22.5 %multiply_add_fusion.2 = (f32[2,32,32,128]{3,2,1,0:T(8,128)}, f32[2,32,32,128]{3,2,1,0:T(8,128)}) fusion(f32[2,32,32,128]{3,2,1,0:T(8,128)} %param.18, f32[2,32,32,128]{3,2,1,0:T(8,128)} %bitcast.179, f32[32,32,128]{2,1,0:T(8,128)} %multiply_multiply_fusion, f32[2,40,40,136]{3,2,1,0:T(8,128)} %select_maximum_fusion.10, ...), kind=kLoop, calls=%fused_computation.292 | loop fusion | flops 8650752 | bytes 29884416 | tf_op jit(solution)/shard_map/add | solution.py:122
  88.7 3.0 copy.110
  97.2 4.1 collective-permute-start.7
  101.3 7.9 %fusion.75 = f32[2,32,32,128]{3,2,1,0:T(8,128)} fusion(f32[2,40,40,136]{3,2,1,0:T(8,128)S(1)} %select_maximum_fusion.14, f32[2,36,32,128]{3,2,1,0:T(8,128)} %copy-done.22, f32[2,36,32,128]{3,2,1,0:T(8,128)} %constant_dynamic-update-slice_fusion, f32[2,32,32,128]{3,2,1,0:T(8,128)S(1)} %copy-done.18, f32[2,32,32,128]{3,2,1,0:T(8,128)} %param.19, ...), kind=kLoop, calls=%fused_computation.263 | loop fusion | flops 8650752 | bytes 28835840 | tf_op jit(solution)/shard_map/add | solution.py:131
  109.2 3.2 copy.112
  112.4 4.8 gather_fusion.3
  124.1 2.5 select_maximum_fusion.8
  127.4 8.2 %multiply_add_fusion.1 = (f32[2,32,32,128]{3,2,1,0:T(8,128)}, f32[2,32,32,128]{3,2,1,0:T(8,128)}) fusion(f32[2,32,32,128]{3,2,1,0:T(8,128)} %bitcast.180, f32[2,32,32,128]{3,2,1,0:T(8,128)} %bitcast.183, f32[32,32,128]{2,1,0:T(8,128)} %multiply_multiply_fusion, f32[2,40,40,136]{3,2,1,0:T(8,128)S(1)} %select_maximum_fusion.8, ...), kind=kLoop, calls=%fused_computation.291 | loop fusion | flops 8650752 | bytes 29884416 | tf_op jit(solution)/shard_map/add | solution.py:122
  142.4 7.1 %gather_fusion.2 = f32[512]{0:T(512)} fusion(f32[2,131072]{1,0:T(2,128)S(1)} %copy-done.16, s32[512]{0:T(512)S(1)} %bitcast.156), kind=kCustom, calls=%fused_computation.2.clone | custom fusion | bytes 8192 | tf_op jit(solution)/shard_map/jit(take_along_axis)/gather | solution.py:124
  150.2 4.8 gather_fusion.1
  155.7 2.6 collective-permute-start.8
  161.9 2.5 select_maximum_fusion.6
  165.1 8.2 %multiply_add_fusion = (f32[2,32,32,128]{3,2,1,0:T(8,128)}, f32[2,32,32,128]{3,2,1,0:T(8,128)}) fusion(f32[2,32,32,128]{3,2,1,0:T(8,128)} %bitcast.184, f32[2,32,32,128]{3,2,1,0:T(8,128)} %bitcast.195, f32[32,32,128]{2,1,0:T(8,128)} %multiply_multiply_fusion, f32[2,40,40,136]{3,2,1,0:T(8,128)S(1)} %select_maximum_fusion.6, ...), kind=kLoop, calls=%fused_computation.290 | loop fusion | flops 8650752 | bytes 29884416 | tf_op jit(solution)/shard_map/add | solution.py:122
  176.9 4.8 gather_fusion
  181.8 24.7 %scatter_fusion.4 = f32[2,131072]{1,0:T(2,128)S(1)} fusion(f32[2,131072]{1,0:T(2,128)S(1)} %bitcast.196, s32[512]{0:T(512)S(1)} %bitcast.151, f32[512]{0:T(512)S(1)} %bitcast.224), kind=kCustom, calls=%fused_computation.8 | custom fusion | flops 512 | bytes 10240 | tf_op jit(solution)/shard_map/scatter-add | solution.py:112
  213.3 3.7 collective-permute-done.10
  219.1 7.8 %fusion.33 = f32[2,32,32,128]{3,2,1,0:T(8,128)} fusion(f32[2,40,40,136]{3,2,1,0:T(8,128)S(1)} %select_maximum_fusion.4, f32[2,36,32,128]{3,2,1,0:T(8,128)} %copy-done.26, f32[2,36,32,128]{3,2,1,0:T(8,128)} %constant_dynamic-update-slice_fusion.20, f32[2,32,32,128]{3,2,1,0:T(8,128)S(1)} %bitcast.162, f32[2,32,32,128]{3,2,1,0:T(8,128)} %param.20, ...), kind=kLoop, calls=%fused_computation.121 | loop fusion | flops 8650752 | bytes 28835840 | tf_op jit(solution)/shard_map/add | solution.py:131
  229.0 24.7 %scatter_fusion.5 = f32[2,131072]{1,0:T(2,128)S(1)} fusion(f32[2,131072]{1,0:T(2,128)S(1)} %bitcast.201, s32[512]{0:T(512)S(1)} %bitcast.152, f32[512]{0:T(512)S(1)} %bitcast.222), kind=kCustom, calls=%fused_computation.9 | custom fusion | flops 512 | bytes 10240 | tf_op jit(solution)/shard_map/scatter-add | solution.py:112
  255.8 2.9 collective-permute-start.12
  260.9 7.2 %collective-permute-done.12 = f32[2,4,32,128]{3,2,1,0:T(8,128)S(1)} collective-permute-done((f32[2,4,32,128]{3,2,1,0:T(8,128)S(1)}, f32[2,4,32,128]{3,2,1,0:T(8,128)S(1)}, u32[]{:S(2)}, u32[]{:S(2)}) %collective-permute-start.12) | collective-permute-done | bytes 131104 | tf_op jit(solution)/shard_map/ppermute | solution.py:20
  270.3 7.8 %fusion.23 = f32[2,32,32,128]{3,2,1,0:T(8,128)} fusion(f32[2,40,40,136]{3,2,1,0:T(8,128)S(1)} %select_maximum_fusion.2, f32[2,36,32,128]{3,2,1,0:T(8,128)} %copy-done.27, f32[2,36,32,128]{3,2,1,0:T(8,128)} %constant_dynamic-update-slice_fusion.24, f32[2,32,32,128]{3,2,1,0:T(8,128)} %bitcast.168, f32[2,32,32,128]{3,2,1,0:T(8,128)S(1)} %bitcast.163, ...), kind=kLoop, calls=%fused_computation.91 | loop fusion | flops 8650752 | bytes 28835840 | tf_op jit(solution)/shard_map/add | solution.py:131
  280.1 24.7 %scatter_fusion.6 = f32[2,131072]{1,0:T(2,128)S(1)} fusion(f32[2,131072]{1,0:T(2,128)S(1)} %bitcast.203, s32[512]{0:T(512)S(1)} %bitcast.153, f32[512]{0:T(512)S(1)} %bitcast.223), kind=kCustom, calls=%fused_computation.10 | custom fusion | flops 512 | bytes 10240 | tf_op jit(solution)/shard_map/scatter-add | solution.py:112
  311.6 3.8 collective-permute-done.14
  317.5 7.9 %fusion.13 = f32[2,32,32,128]{3,2,1,0:T(8,128)} fusion(f32[2,40,40,136]{3,2,1,0:T(8,128)S(1)} %select_maximum_fusion, f32[2,36,32,128]{3,2,1,0:T(8,128)} %copy-done.28, f32[2,36,32,128]{3,2,1,0:T(8,128)} %constant_dynamic-update-slice_fusion.28, f32[2,32,32,128]{3,2,1,0:T(8,128)} %bitcast.174, f32[2,32,32,128]{3,2,1,0:T(8,128)S(1)} %bitcast.169, ...), kind=kLoop, calls=%fused_computation.61 | loop fusion | flops 8650752 | bytes 28835840 | tf_op jit(solution)/shard_map/add | solution.py:131
  325.4 3.0 copy.105
  328.4 70.2 %scatter_fusion.7 = f32[2,131072]{1,0:T(2,128)} fusion(f32[2,131072]{1,0:T(2,128)} %bitcast.199, s32[512]{0:T(512)S(1)} %bitcast.154, f32[512]{0:T(512)S(1)} %bitcast.221), kind=kCustom, calls=%fused_computation.11 | custom fusion | flops 512 | bytes 10240 | tf_op jit(solution)/shard_map/scatter-add | solution.py:112
  400.0 3.3 add_reduce_fusion
  404.2 2.9 copy.45
  408.8 9.5 %all-to-all-start.1 = ((f32[16,1,8192]{2,1,0:T(1,128)}), f32[16,1,8192]{2,1,0:T(1,128)S(1)}, u32[]{:S(2)}, u32[]{:S(2)}) async-start(f32[16,1,8192]{2,1,0:T(1,128)} %reshape.253), calls=%async_computation.1 | async-start | bytes 1048576 | tf_op jit(solution)/shard_map/all_to_all | solution.py:142
  418.4 75.7 %all-reduce.10.cloned.1.call-done = f32[32,32,128]{2,1,0:T(8,128)} async-done(((f32[32,32,128]{2,1,0:T(8,128)}), f32[32,32,128]{2,1,0:T(8,128)}) %all-reduce.10.cloned.1.call-update) | async-done | bytes 524304 | tf_op jit(solution)/shard_map/psum | solution.py:139
  494.1 2.9 copy.42
  498.7 10.7 %all-to-all-start = ((f32[16,1,8192]{2,1,0:T(1,128)}), f32[16,1,8192]{2,1,0:T(1,128)}, u32[]{:S(2)}, u32[]{:S(2)}) async-start(f32[16,1,8192]{2,1,0:T(1,128)} %reshape.255), calls=%async_computation | async-start | bytes 1048576 | tf_op jit(solution)/shard_map/all_to_all | solution.py:141
  513.2 2.7 copy.47
  518.2 4.8 convolution_multiply_fusion
  523.1 3.0 reduce.9
  526.7 2.7 copy.44
  529.4 2.5 reshape.131
  531.9 4.8 fusion.4
  536.8 5.1 convolution_bitcast_fusion
  544.4 6.0 %all-to-all-start.2 = ((f32[16,1,8192]{2,1,0:T(1,128)}), f32[16,1,8192]{2,1,0:T(1,128)S(1)}, u32[]{:S(2)}, u32[]{:S(2)}) async-start(f32[16,1,8192]{2,1,0:T(1,128)} %reshape.257), calls=%async_computation.2 | async-start | bytes 1048576 | tf_op jit(solution)/shard_map/all_to_all | solution.py:145
  550.8 9.5 %all-to-all-done.2 = f32[16,1,8192]{2,1,0:T(1,128)S(1)} async-done(((f32[16,1,8192]{2,1,0:T(1,128)}), f32[16,1,8192]{2,1,0:T(1,128)S(1)}, u32[]{:S(2)}, u32[]{:S(2)}) %all-to-all-start.2) | async-done | bytes 524320 | tf_op jit(solution)/shard_map/all_to_all | solution.py:145
  (202 shorter events, 106.7 us)
Async XLA Ops:
  6.5 487.5 %all-reduce.10.cloned.1.call-start = ((), (), s32[]{:S(2)}) async-start(), calls=%async_computation.3 | async-start | bytes 1048576 | tf_op jit(solution)/shard_map/psum | solution.py:139
  7.5 22.4 %collective-permute-start.3 = (f32[2,4,32,128]{3,2,1,0:T(8,128)S(1)}, f32[2,4,32,128]{3,2,1,0:T(8,128)S(1)}, u32[]{:S(2)}, u32[]{:S(2)}) collective-permute-start(f32[2,4,32,128]{3,2,1,0:T(8,128)S(1)} %get-tuple-element.46), channel_id=1, source_target_pairs={{0,1},{1,2},{2,3},{3,4},{4,5},{5,6},{6,7},{7,8},{8,9},{9,10},{10,1... | collective-permute-start | bytes 393224 | tf_op jit(solution)/shard_map/ppermute | solution.py:17
  12.1 21.3 %collective-permute-start.2 = (f32[2,4,32,128]{3,2,1,0:T(8,128)S(1)}, f32[2,4,32,128]{3,2,1,0:T(8,128)}, u32[]{:S(2)}, u32[]{:S(2)}) collective-permute-start(f32[2,4,32,128]{3,2,1,0:T(8,128)S(1)} %get-tuple-element.47), channel_id=1, source_target_pairs={{1,0},{2,1},{3,2},{4,3},{5,4},{6,5},{7,6},{8,7},{9,8},{10,9},{11,1... | collective-permute-start | bytes 393224 | tf_op jit(solution)/shard_map/ppermute | solution.py:20
  15.7 40.3 %collective-permute-start.1 = (f32[2,4,32,128]{3,2,1,0:T(8,128)}, f32[2,4,32,128]{3,2,1,0:T(8,128)S(1)}, u32[]{:S(2)}, u32[]{:S(2)}) collective-permute-start(f32[2,4,32,128]{3,2,1,0:T(8,128)} %get-tuple-element.50), channel_id=1, source_target_pairs={{0,1},{1,2},{2,3},{3,4},{4,5},{5,6},{6,7},{7,8},{8,9},{9,10},{10,1... | collective-permute-start | bytes 393224 | tf_op jit(solution)/shard_map/ppermute | solution.py:17
  19.4 36.7 %collective-permute-start = (f32[2,4,32,128]{3,2,1,0:T(8,128)}, f32[2,4,32,128]{3,2,1,0:T(8,128)S(1)}, u32[]{:S(2)}, u32[]{:S(2)}) collective-permute-start(f32[2,4,32,128]{3,2,1,0:T(8,128)} %get-tuple-element.51), channel_id=1, source_target_pairs={{1,0},{2,1},{3,2},{4,3},{5,4},{6,5},{7,6},{8,7},{9,8},{10,9},{11,1... | collective-permute-start | bytes 393224 | tf_op jit(solution)/shard_map/ppermute | solution.py:20
  25.8 7.6 %copy-start.19 = (f32[2,32,32,128]{3,2,1,0:T(8,128)S(1)}, f32[2,32,32,128]{3,2,1,0:T(8,128)}, u32[]{:S(2)}) copy-start(f32[2,32,32,128]{3,2,1,0:T(8,128)} %param.18) | copy-start | bytes 3145732
  49.6 9.1 %copy-start.17 = (f32[2,32,32,128]{3,2,1,0:T(8,128)S(1)}, f32[2,32,32,128]{3,2,1,0:T(8,128)}, u32[]{:S(2)}) copy-start(f32[2,32,32,128]{3,2,1,0:T(8,128)} %param.20) | copy-start | bytes 3145732
  49.7 13.3 %copy-start.11 = (f32[1,2,1024,128]{3,2,1,0:T(8,128)}, f32[1,2,1024,128]{3,2,1,0:T(8,128)S(1)}, u32[]{:S(2)}) copy-start(f32[1,2,1024,128]{3,2,1,0:T(8,128)S(1)} %copy.61) | copy-start | bytes 3145732
  49.7 10.9 %collective-permute-start.5 = (f32[2,4,32,128]{3,2,1,0:T(8,128)S(1)}, f32[2,4,32,128]{3,2,1,0:T(8,128)S(1)}, u32[]{:S(2)}, u32[]{:S(2)}) collective-permute-start(f32[2,4,32,128]{3,2,1,0:T(8,128)S(1)} %get-tuple-element.42), channel_id=1, source_target_pairs={{0,1},{1,2},{2,3},{3,4},{4,5},{5,6},{6,7},{7,8},{8,9},{9,10},{10,1... | collective-permute-start | bytes 393224 | tf_op jit(solution)/shard_map/ppermute | solution.py:17
  53.6 9.3 %collective-permute-start.4 = (f32[2,4,32,128]{3,2,1,0:T(8,128)S(1)}, f32[2,4,32,128]{3,2,1,0:T(8,128)S(1)}, u32[]{:S(2)}, u32[]{:S(2)}) collective-permute-start(f32[2,4,32,128]{3,2,1,0:T(8,128)S(1)} %get-tuple-element.43), channel_id=1, source_target_pairs={{1,0},{2,1},{3,2},{4,3},{5,4},{6,5},{7,6},{8,7},{9,8},{10,9},{11,1... | collective-permute-start | bytes 393224 | tf_op jit(solution)/shard_map/ppermute | solution.py:20
  94.1 7.2 %copy-start.18 = (f32[2,32,32,128]{3,2,1,0:T(8,128)S(1)}, f32[2,32,32,128]{3,2,1,0:T(8,128)}, u32[]{:S(2)}) copy-start(f32[2,32,32,128]{3,2,1,0:T(8,128)} %param.20) | copy-start | bytes 3145732
  97.2 22.8 %collective-permute-start.7 = (f32[2,4,32,128]{3,2,1,0:T(8,128)}, f32[2,4,32,128]{3,2,1,0:T(8,128)S(1)}, u32[]{:S(2)}, u32[]{:S(2)}) collective-permute-start(f32[2,4,32,128]{3,2,1,0:T(8,128)} %get-tuple-element.38), channel_id=1, source_target_pairs={{0,1},{1,2},{2,3},{3,4},{4,5},{5,6},{6,7},{7,8},{8,9},{9,10},{10,1... | collective-permute-start | bytes 393224 | tf_op jit(solution)/shard_map/ppermute | solution.py:17
  109.2 10.8 %copy-start.13 = (f32[1,2,1024,128]{3,2,1,0:T(8,128)S(1)}, f32[1,2,1024,128]{3,2,1,0:T(8,128)}, u32[]{:S(2)}) copy-start(f32[1,2,1024,128]{3,2,1,0:T(8,128)} %copy-done.12) | copy-start | bytes 3145732
  117.9 6.3 %collective-permute-start.6 = (f32[2,4,32,128]{3,2,1,0:T(8,128)S(1)}, f32[2,4,32,128]{3,2,1,0:T(8,128)S(1)}, u32[]{:S(2)}, u32[]{:S(2)}) collective-permute-start(f32[2,4,32,128]{3,2,1,0:T(8,128)S(1)} %get-tuple-element.39), channel_id=1, source_target_pairs={{1,0},{2,1},{3,2},{4,3},{5,4},{6,5},{7,6},{8,7},{9,8},{10,9},{11,1... | collective-permute-start | bytes 393224 | tf_op jit(solution)/shard_map/ppermute | solution.py:20
  127.3 10.3 %copy-start.40 = (f32[16]{0:T(128)S(1)}, f32[16]{0:T(128)}, u32[]{:S(2)}) copy-start(f32[16]{0:T(128)} %reshape.175) | copy-start | bytes 196
  135.6 6.9 %copy-start.16 = (f32[2,131072]{1,0:T(2,128)S(1)}, f32[2,131072]{1,0:T(2,128)}, u32[]{:S(2)}) copy-start(f32[2,131072]{1,0:T(2,128)} %scatter_fusion.1) | copy-start | bytes 3145732
  139.1 20.3 %copy-start.20 = (f32[1,2,1024,128]{3,2,1,0:T(8,128)}, f32[1,2,1024,128]{3,2,1,0:T(8,128)S(1)}, u32[]{:S(2)}) copy-start(f32[1,2,1024,128]{3,2,1,0:T(8,128)S(1)} %copy.65) | copy-start | bytes 3145732
  139.2 19.1 %collective-permute-start.9 = (f32[2,4,32,128]{3,2,1,0:T(8,128)S(1)}, f32[2,4,32,128]{3,2,1,0:T(8,128)S(1)}, u32[]{:S(2)}, u32[]{:S(2)}) collective-permute-start(f32[2,4,32,128]{3,2,1,0:T(8,128)S(1)} %get-tuple-element.34), channel_id=1, source_target_pairs={{0,1},{1,2},{2,3},{3,4},{4,5},{5,6},{6,7},{7,8},{8,9},{9,10},{10,1... | collective-permute-start | bytes 393224 | tf_op jit(solution)/shard_map/ppermute | solution.py:17
  155.7 6.3 %collective-permute-start.8 = (f32[2,4,32,128]{3,2,1,0:T(8,128)S(1)}, f32[2,4,32,128]{3,2,1,0:T(8,128)S(1)}, u32[]{:S(2)}, u32[]{:S(2)}) collective-permute-start(f32[2,4,32,128]{3,2,1,0:T(8,128)S(1)} %get-tuple-element.35), channel_id=1, source_target_pairs={{1,0},{2,1},{3,2},{4,3},{5,4},{6,5},{7,6},{8,7},{9,8},{10,9},{11,1... | collective-permute-start | bytes 393224 | tf_op jit(solution)/shard_map/ppermute | solution.py:20
  165.1 10.4 %copy-start.39 = (f32[16]{0:T(128)S(1)}, f32[16]{0:T(128)}, u32[]{:S(2)}) copy-start(f32[16]{0:T(128)} %reshape.181) | copy-start | bytes 196
  173.3 8.4 %copy-start.34 = (f32[2,256]{1,0:T(2,128)S(1)}, f32[2,256]{1,0:T(2,128)}, u32[]{:S(2)}) copy-start(f32[2,256]{1,0:T(2,128)} %reshape.238) | copy-start | bytes 6148
  173.4 8.4 %copy-start.35 = (f32[2,1,256]{2,1,0:T(1,128)S(1)}, f32[2,1,256]{2,1,0:T(1,128)}, u32[]{:S(2)}) copy-start(f32[2,1,256]{2,1,0:T(1,128)} %get-tuple-element.52) | copy-start | bytes 6148
  173.4 8.4 %copy-start.36 = (f32[2,1,256]{2,1,0:T(1,128)S(1)}, f32[2,1,256]{2,1,0:T(1,128)}, u32[]{:S(2)}) copy-start(f32[2,1,256]{2,1,0:T(1,128)} %get-tuple-element.53) | copy-start | bytes 6148
  173.4 8.4 %copy-start.37 = (f32[2,1,256]{2,1,0:T(1,128)S(1)}, f32[2,1,256]{2,1,0:T(1,128)}, u32[]{:S(2)}) copy-start(f32[2,1,256]{2,1,0:T(1,128)} %get-tuple-element.55) | copy-start | bytes 6148
  173.4 8.4 %copy-start.38 = (pred[2,256]{1,0:T(4,128)(4,1)S(1)}, pred[2,256]{1,0:T(4,128)(4,1)}, u32[]{:S(2)}) copy-start(pred[2,256]{1,0:T(4,128)(4,1)} %get-tuple-element.11) | copy-start | bytes 1540
  173.4 8.4 %copy-start.21 = (f32[1,2,1024,128]{3,1,2,0:T(2,128)S(1)}, f32[1,2,1024,128]{3,1,2,0:T(2,128)}, u32[]{:S(2)}) copy-start(f32[1,2,1024,128]{3,1,2,0:T(2,128)} %copy.112) | copy-start | bytes 3145732
  206.7 12.5 %copy-start.3 = (f32[1,2,1024,128]{3,2,1,0:T(8,128)}, f32[1,2,1024,128]{3,2,1,0:T(8,128)S(1)}, u32[]{:S(2)}) copy-start(f32[1,2,1024,128]{3,2,1,0:T(8,128)S(1)} %copy.69) | copy-start | bytes 3145732
  206.7 4.4 collective-permute-start.11
  208.6 8.4 %collective-permute-start.10 = (f32[2,4,32,128]{3,2,1,0:T(8,128)S(1)}, f32[2,4,32,128]{3,2,1,0:T(8,128)S(1)}, u32[]{:S(2)}, u32[]{:S(2)}) collective-permute-start(f32[2,4,32,128]{3,2,1,0:T(8,128)S(1)} %get-tuple-element.31), channel_id=1, source_target_pairs={{1,0},{2,1},{3,2},{4,3},{5,4},{6,5},{7,6},{8,7},{9,8},{10,9},{11,1... | collective-permute-start | bytes 393224 | tf_op jit(solution)/shard_map/ppermute | solution.py:20
  211.1 8.1 %copy-start = (f32[32,32,128]{2,1,0:T(8,128)S(1)}, f32[32,32,128]{2,1,0:T(8,128)}, u32[]{:S(2)}) copy-start(f32[32,32,128]{2,1,0:T(8,128)} %multiply_multiply_fusion) | copy-start | bytes 1572868
  253.8 15.8 %copy-start.6 = (f32[1,2,1024,128]{3,2,1,0:T(8,128)}, f32[1,2,1024,128]{3,2,1,0:T(8,128)S(1)}, u32[]{:S(2)}) copy-start(f32[1,2,1024,128]{3,2,1,0:T(8,128)S(1)} %copy.72) | copy-start | bytes 3145732
  253.9 4.8 collective-permute-start.13
  255.8 12.4 %collective-permute-start.12 = (f32[2,4,32,128]{3,2,1,0:T(8,128)S(1)}, f32[2,4,32,128]{3,2,1,0:T(8,128)S(1)}, u32[]{:S(2)}, u32[]{:S(2)}) collective-permute-start(f32[2,4,32,128]{3,2,1,0:T(8,128)S(1)} %get-tuple-element.27), channel_id=1, source_target_pairs={{1,0},{2,1},{3,2},{4,3},{5,4},{6,5},{7,6},{8,7},{9,8},{10,9},{11,1... | collective-permute-start | bytes 393224 | tf_op jit(solution)/shard_map/ppermute | solution.py:20
  258.7 11.6 %copy-start.1 = (f32[32,32,128]{2,1,0:T(8,128)S(1)}, f32[32,32,128]{2,1,0:T(8,128)}, u32[]{:S(2)}) copy-start(f32[32,32,128]{2,1,0:T(8,128)} %multiply_multiply_fusion) | copy-start | bytes 1572868
  258.7 11.6 %copy-start.4 = (f32[1,2,1024,128]{3,2,1,0:T(8,128)S(1)}, f32[1,2,1024,128]{3,2,1,0:T(8,128)}, u32[]{:S(2)}) copy-start(f32[1,2,1024,128]{3,2,1,0:T(8,128)} %copy-done.3) | copy-start | bytes 3145732
  280.1 26.9 %copy-start.33 = (f32[1,2,2,128]{3,2,1,0:T(2,128)S(1)}, f32[1,2,2,128]{3,2,1,0:T(2,128)}, u32[]{:S(2)}) copy-start(f32[1,2,2,128]{3,2,1,0:T(2,128)} %get-tuple-element.10) | copy-start | bytes 6148
  305.0 11.9 %copy-start.9 = (f32[1,2,1024,128]{3,2,1,0:T(8,128)}, f32[1,2,1024,128]{3,2,1,0:T(8,128)S(1)}, u32[]{:S(2)}) copy-start(f32[1,2,1024,128]{3,2,1,0:T(8,128)S(1)} %copy.75) | copy-start | bytes 3145732
  305.0 4.4 collective-permute-start.15
  307.1 8.3 %collective-permute-start.14 = (f32[2,4,32,128]{3,2,1,0:T(8,128)S(1)}, f32[2,4,32,128]{3,2,1,0:T(8,128)S(1)}, u32[]{:S(2)}, u32[]{:S(2)}) collective-permute-start(f32[2,4,32,128]{3,2,1,0:T(8,128)S(1)} %get-tuple-element.23), channel_id=1, source_target_pairs={{1,0},{2,1},{3,2},{4,3},{5,4},{6,5},{7,6},{8,7},{9,8},{10,9},{11,1... | collective-permute-start | bytes 393224 | tf_op jit(solution)/shard_map/ppermute | solution.py:20
  309.4 8.1 %copy-start.2 = (f32[32,32,128]{2,1,0:T(8,128)S(1)}, f32[32,32,128]{2,1,0:T(8,128)}, u32[]{:S(2)}) copy-start(f32[32,32,128]{2,1,0:T(8,128)} %multiply_multiply_fusion) | copy-start | bytes 1572868
  309.4 8.1 %copy-start.7 = (f32[1,2,1024,128]{3,2,1,0:T(8,128)S(1)}, f32[1,2,1024,128]{3,2,1,0:T(8,128)}, u32[]{:S(2)}) copy-start(f32[1,2,1024,128]{3,2,1,0:T(8,128)} %copy-done.6) | copy-start | bytes 3145732
  328.4 71.5 %copy-start.5 = (f32[1,2,1024,128]{3,2,1,0:T(8,128)S(1)}, f32[1,2,1024,128]{3,2,1,0:T(8,128)}, u32[]{:S(2)}) copy-start(f32[1,2,1024,128]{3,2,1,0:T(8,128)} %copy-done.3) | copy-start | bytes 3145732
  328.4 71.5 %copy-start.8 = (f32[1,2,1024,128]{3,2,1,0:T(8,128)S(1)}, f32[1,2,1024,128]{3,2,1,0:T(8,128)}, u32[]{:S(2)}) copy-start(f32[1,2,1024,128]{3,2,1,0:T(8,128)} %copy-done.6) | copy-start | bytes 3145732
  328.4 71.5 %copy-start.10 = (f32[1,2,1024,128]{3,2,1,0:T(8,128)S(1)}, f32[1,2,1024,128]{3,2,1,0:T(8,128)}, u32[]{:S(2)}) copy-start(f32[1,2,1024,128]{3,2,1,0:T(8,128)} %copy-done.9) | copy-start | bytes 3145732
  408.8 89.8 %all-to-all-start.1 = ((f32[16,1,8192]{2,1,0:T(1,128)}), f32[16,1,8192]{2,1,0:T(1,128)S(1)}, u32[]{:S(2)}, u32[]{:S(2)}) async-start(f32[16,1,8192]{2,1,0:T(1,128)} %reshape.253), calls=%async_computation.1 | async-start | bytes 1048576 | tf_op jit(solution)/shard_map/all_to_all | solution.py:142
  498.7 24.4 %all-to-all-start = ((f32[16,1,8192]{2,1,0:T(1,128)}), f32[16,1,8192]{2,1,0:T(1,128)}, u32[]{:S(2)}, u32[]{:S(2)}) async-start(f32[16,1,8192]{2,1,0:T(1,128)} %reshape.255), calls=%async_computation | async-start | bytes 1048576 | tf_op jit(solution)/shard_map/all_to_all | solution.py:141
  541.8 8.5 %copy-start.30 = (f32[32,32,128]{2,1,0:T(8,128)S(1)}, f32[32,32,128]{2,1,0:T(8,128)}, u32[]{:S(2)}) copy-start(f32[32,32,128]{2,1,0:T(8,128)} %param.14) | copy-start | bytes 1572868
  544.4 15.9 %all-to-all-start.2 = ((f32[16,1,8192]{2,1,0:T(1,128)}), f32[16,1,8192]{2,1,0:T(1,128)S(1)}, u32[]{:S(2)}, u32[]{:S(2)}) async-start(f32[16,1,8192]{2,1,0:T(1,128)} %reshape.257), calls=%async_computation.2 | async-start | bytes 1048576 | tf_op jit(solution)/shard_map/all_to_all | solution.py:145
  (13 other events, 34.1 us)
Sparse Core Ops, SparseCore 0:
  404.4 89.6 all-reduce.9
where the time goes:
time: 578 us; the launch traced here: 571 us
  other arithmetic  264 us (46%)
  local copies, waits for them, and re-layouts  105 us (18%)
  waiting for transfers between devices  103 us (18%)
  starting transfers between devices  68.8 us (12%)
  between operations  15.5 us (3%)
  matrix products  14.7 us (3%)
    scatter-add x8, other arithmetic, place(): flat.at[rows_full, target].add(values, mode='drop').reshape(field.shape)  151 us
    psum x1, waiting for transfers between devices, body(): total = lax.psum(partial_value, 'shot')  75.7 us
    unnamed x127, local copies, waits for them, and re-layouts  52 us
    add x4, other arithmetic, body(): advanced = 2.0 * current - prior + speed_sq * spread  47.2 us
    add x4, other arithmetic, body(): earlier = 2.0 * adj_current - adj_later + speed_sq * spread  31.4 us
    ppermute x8, starting transfers between devices, extended(): lax.ppermute(lax.slice_in_dim(block, block.shape[dim] - width, None, axis...  24 us
    gather x8, local copies, waits for them, and re-layouts, body(): jnp.take_along_axis(advanced.reshape(shots_here, -1), record_clip, axis=1)  23.5 us
    ppermute x8, starting transfers between devices, extended(): lax.ppermute(lax.slice_in_dim(block, 0, width, axis=dim), axis, backward)  18.6 us
  transfers between devices with their start and end apart: 20, of which 7 were waited for; matrix products, arithmetic and copies ran while one was open for 17% of the time, Pallas kernels for 0%

commit v1 on v0

--- a/solution.py
+++ b/solution.py
@@ -136,7 +136,7 @@
     rate = step_size[0]
     shot_rows = velocity.shape[2] // lax.axis_size("shot")
     start = lax.axis_index("shot") * shot_rows
-    total = lax.psum(partial_value, "shot")
+    total = jnp.sum(lax.all_gather(partial_value, "shot"), axis=0)
     grad_cols, noise_cols = (
         lax.all_to_all(total, "dom", split_axis=2, concat_axis=0, tiled=True),
         lax.all_to_all(noise_field, "dom", split_axis=2, concat_axis=0, tiled=True),

time: 578 us -> 564 us (0.976)
  waiting for transfers between devices: 103 us -> 92.4 us
    psum x1 -> x0, waiting for transfers between devices: 75.7 us -> none  [body(): total = lax.psum(partial_value, 'shot')]
    all_gather x0 -> x1, waiting for transfers between devices: none -> 64.8 us  [body(): total = jnp.sum(lax.all_gather(partial_value, 'shot'), axis=0)]
where the time goes in v1:
time: 564 us; the launch traced here: 557 us
  other arithmetic  267 us (47%)
  local copies, waits for them, and re-layouts  104 us (18%)
  waiting for transfers between devices  92.4 us (16%)
  starting transfers between devices  63.9 us (11%)
  between operations  15.5 us (3%)
  matrix products  14.7 us (3%)
    scatter-add x8, other arithmetic, place(): flat.at[rows_full, target].add(values, mode='drop').reshape(field.shape)  151 us
    all_gather x1, waiting for transfers between devices, body(): total = jnp.sum(lax.all_gather(partial_value, 'shot'), axis=0)  64.8 us
    unnamed x127, local copies, waits for them, and re-layouts  52 us
    add x4, other arithmetic, body(): advanced = 2.0 * current - prior + speed_sq * spread  47.2 us
    add x4, other arithmetic, body(): earlier = 2.0 * adj_current - adj_later + speed_sq * spread  31.4 us
    ppermute x8, starting transfers between devices, extended(): lax.ppermute(lax.slice_in_dim(block, block.shape[dim] - width, None, axis...  24 us
    gather x8, local copies, waits for them, and re-layouts, body(): jnp.take_along_axis(advanced.reshape(shots_here, -1), record_clip, axis=1)  23.5 us
    ppermute x8, starting transfers between devices, extended(): lax.ppermute(lax.slice_in_dim(block, 0, width, axis=dim), axis, backward)  18.6 us
  transfers between devices with their start and end apart: 20, of which 7 were waited for; matrix products, arithmetic and copies ran while one was open for 17% of the time, Pallas kernels for 0%

profile of v1, /device:TPU:1, one launch (start us, length us, event | category | flops | bytes accessed | tf_op | source)
XLA Modules:
  0.0 556.8 jit_solution(459686251768567726)
XLA Ops:
  7.5 4.6 collective-permute-start.3
  15.7 3.6 collective-permute-start.1
  37.4 8.3 %multiply_add_fusion.3 = (f32[2,32,32,128]{3,2,1,0:T(8,128)}, f32[2,32,32,128]{3,2,1,0:T(8,128)}) fusion(f32[2,32,32,128]{3,2,1,0:T(8,128)} %param.17, f32[2,32,32,128]{3,2,1,0:T(8,128)} %param.18, f32[32,32,128]{2,1,0:T(8,128)} %multiply_multiply_fusion, f32[2,40,40,136]{3,2,1,0:T(8,128)S(1)} %select_maximum_fusion.12, f32[2,36,32,128]{3,2,1,0:T(8,128)} %copy-done.23, ...), kind=kLoop, calls=%fused_computation.293 | loop fusion | flops 8650752 | bytes 29884416 | tf_op jit(solution)/shard_map/add | solution.py:122
  49.7 3.9 collective-permute-start.5
  53.6 2.4 collective-permute-start.4
  56.1 2.5 select_maximum_fusion.14
  62.9 2.6 select_maximum_fusion.10
  66.2 22.5 %multiply_add_fusion.2 = (f32[2,32,32,128]{3,2,1,0:T(8,128)}, f32[2,32,32,128]{3,2,1,0:T(8,128)}) fusion(f32[2,32,32,128]{3,2,1,0:T(8,128)} %param.18, f32[2,32,32,128]{3,2,1,0:T(8,128)} %bitcast.180, f32[32,32,128]{2,1,0:T(8,128)} %multiply_multiply_fusion, f32[2,40,40,136]{3,2,1,0:T(8,128)} %select_maximum_fusion.10, ...), kind=kLoop, calls=%fused_computation.292 | loop fusion | flops 8650752 | bytes 29884416 | tf_op jit(solution)/shard_map/add | solution.py:122
  88.7 3.0 copy.109
  97.2 4.1 collective-permute-start.7
  101.3 7.9 %fusion.75 = f32[2,32,32,128]{3,2,1,0:T(8,128)} fusion(f32[2,40,40,136]{3,2,1,0:T(8,128)S(1)} %select_maximum_fusion.14, f32[2,36,32,128]{3,2,1,0:T(8,128)} %copy-done.22, f32[2,36,32,128]{3,2,1,0:T(8,128)} %constant_dynamic-update-slice_fusion, f32[2,32,32,128]{3,2,1,0:T(8,128)S(1)} %copy-done.18, f32[2,32,32,128]{3,2,1,0:T(8,128)} %param.19, ...), kind=kLoop, calls=%fused_computation.263 | loop fusion | flops 8650752 | bytes 28835840 | tf_op jit(solution)/shard_map/add | solution.py:131
  109.2 3.2 copy.111
  112.4 4.8 gather_fusion.3
  124.1 2.5 select_maximum_fusion.8
  127.4 8.2 %multiply_add_fusion.1 = (f32[2,32,32,128]{3,2,1,0:T(8,128)}, f32[2,32,32,128]{3,2,1,0:T(8,128)}) fusion(f32[2,32,32,128]{3,2,1,0:T(8,128)} %bitcast.181, f32[2,32,32,128]{3,2,1,0:T(8,128)} %bitcast.184, f32[32,32,128]{2,1,0:T(8,128)} %multiply_multiply_fusion, f32[2,40,40,136]{3,2,1,0:T(8,128)S(1)} %select_maximum_fusion.8, ...), kind=kLoop, calls=%fused_computation.291 | loop fusion | flops 8650752 | bytes 29884416 | tf_op jit(solution)/shard_map/add | solution.py:122
  142.4 7.1 %gather_fusion.2 = f32[512]{0:T(512)} fusion(f32[2,131072]{1,0:T(2,128)S(1)} %copy-done.16, s32[512]{0:T(512)S(1)} %bitcast.157), kind=kCustom, calls=%fused_computation.2.clone | custom fusion | bytes 8192 | tf_op jit(solution)/shard_map/jit(take_along_axis)/gather | solution.py:124
  150.2 4.8 gather_fusion.1
  155.7 2.6 collective-permute-start.8
  161.9 2.5 select_maximum_fusion.6
  165.1 8.2 %multiply_add_fusion = (f32[2,32,32,128]{3,2,1,0:T(8,128)}, f32[2,32,32,128]{3,2,1,0:T(8,128)}) fusion(f32[2,32,32,128]{3,2,1,0:T(8,128)} %bitcast.185, f32[2,32,32,128]{3,2,1,0:T(8,128)} %bitcast.196, f32[32,32,128]{2,1,0:T(8,128)} %multiply_multiply_fusion, f32[2,40,40,136]{3,2,1,0:T(8,128)S(1)} %select_maximum_fusion.6, ...), kind=kLoop, calls=%fused_computation.290 | loop fusion | flops 8650752 | bytes 29884416 | tf_op jit(solution)/shard_map/add | solution.py:122
  176.9 4.8 gather_fusion
  181.8 24.7 %scatter_fusion.4 = f32[2,131072]{1,0:T(2,128)S(1)} fusion(f32[2,131072]{1,0:T(2,128)S(1)} %bitcast.197, s32[512]{0:T(512)S(1)} %bitcast.152, f32[512]{0:T(512)S(1)} %bitcast.226), kind=kCustom, calls=%fused_computation.8 | custom fusion | flops 512 | bytes 10240 | tf_op jit(solution)/shard_map/scatter-add | solution.py:112
  213.3 3.7 collective-permute-done.10
  219.1 7.8 %fusion.33 = f32[2,32,32,128]{3,2,1,0:T(8,128)} fusion(f32[2,40,40,136]{3,2,1,0:T(8,128)S(1)} %select_maximum_fusion.4, f32[2,36,32,128]{3,2,1,0:T(8,128)} %copy-done.26, f32[2,36,32,128]{3,2,1,0:T(8,128)} %constant_dynamic-update-slice_fusion.20, f32[2,32,32,128]{3,2,1,0:T(8,128)S(1)} %bitcast.163, f32[2,32,32,128]{3,2,1,0:T(8,128)} %param.20, ...), kind=kLoop, calls=%fused_computation.121 | loop fusion | flops 8650752 | bytes 28835840 | tf_op jit(solution)/shard_map/add | solution.py:131
  229.0 24.7 %scatter_fusion.5 = f32[2,131072]{1,0:T(2,128)S(1)} fusion(f32[2,131072]{1,0:T(2,128)S(1)} %bitcast.202, s32[512]{0:T(512)S(1)} %bitcast.153, f32[512]{0:T(512)S(1)} %bitcast.224), kind=kCustom, calls=%fused_computation.9 | custom fusion | flops 512 | bytes 10240 | tf_op jit(solution)/shard_map/scatter-add | solution.py:112
  255.8 2.9 collective-permute-start.12
  260.9 7.2 %collective-permute-done.12 = f32[2,4,32,128]{3,2,1,0:T(8,128)S(1)} collective-permute-done((f32[2,4,32,128]{3,2,1,0:T(8,128)S(1)}, f32[2,4,32,128]{3,2,1,0:T(8,128)S(1)}, u32[]{:S(2)}, u32[]{:S(2)}) %collective-permute-start.12) | collective-permute-done | bytes 131104 | tf_op jit(solution)/shard_map/ppermute | solution.py:20
  270.3 7.8 %fusion.23 = f32[2,32,32,128]{3,2,1,0:T(8,128)} fusion(f32[2,40,40,136]{3,2,1,0:T(8,128)S(1)} %select_maximum_fusion.2, f32[2,36,32,128]{3,2,1,0:T(8,128)} %copy-done.27, f32[2,36,32,128]{3,2,1,0:T(8,128)} %constant_dynamic-update-slice_fusion.24, f32[2,32,32,128]{3,2,1,0:T(8,128)} %bitcast.169, f32[2,32,32,128]{3,2,1,0:T(8,128)S(1)} %bitcast.164, ...), kind=kLoop, calls=%fused_computation.91 | loop fusion | flops 8650752 | bytes 28835840 | tf_op jit(solution)/shard_map/add | solution.py:131
  280.1 24.7 %scatter_fusion.6 = f32[2,131072]{1,0:T(2,128)S(1)} fusion(f32[2,131072]{1,0:T(2,128)S(1)} %bitcast.204, s32[512]{0:T(512)S(1)} %bitcast.154, f32[512]{0:T(512)S(1)} %bitcast.225), kind=kCustom, calls=%fused_computation.10 | custom fusion | flops 512 | bytes 10240 | tf_op jit(solution)/shard_map/scatter-add | solution.py:112
  311.6 3.8 collective-permute-done.14
  317.5 7.9 %fusion.13 = f32[2,32,32,128]{3,2,1,0:T(8,128)} fusion(f32[2,40,40,136]{3,2,1,0:T(8,128)S(1)} %select_maximum_fusion, f32[2,36,32,128]{3,2,1,0:T(8,128)} %copy-done.28, f32[2,36,32,128]{3,2,1,0:T(8,128)} %constant_dynamic-update-slice_fusion.28, f32[2,32,32,128]{3,2,1,0:T(8,128)} %bitcast.175, f32[2,32,32,128]{3,2,1,0:T(8,128)S(1)} %bitcast.170, ...), kind=kLoop, calls=%fused_computation.61 | loop fusion | flops 8650752 | bytes 28835840 | tf_op jit(solution)/shard_map/add | solution.py:131
  325.4 3.0 copy.104
  328.4 70.2 %scatter_fusion.7 = f32[2,131072]{1,0:T(2,128)} fusion(f32[2,131072]{1,0:T(2,128)} %bitcast.200, s32[512]{0:T(512)S(1)} %bitcast.155, f32[512]{0:T(512)S(1)} %bitcast.223), kind=kCustom, calls=%fused_computation.11 | custom fusion | flops 512 | bytes 10240 | tf_op jit(solution)/shard_map/scatter-add | solution.py:112
  400.0 3.3 add_reduce_fusion
  404.3 2.9 copy.44
  408.9 9.5 %all-to-all-start.1 = ((f32[16,1,8192]{2,1,0:T(1,128)}), f32[16,1,8192]{2,1,0:T(1,128)S(1)}, u32[]{:S(2)}, u32[]{:S(2)}) async-start(f32[16,1,8192]{2,1,0:T(1,128)} %reshape.254), calls=%async_computation.1 | async-start | bytes 1048576 | tf_op jit(solution)/shard_map/all_to_all | solution.py:142
  418.4 64.8 %all-gather.3.cloned.1.call-done = f32[256,32,128]{2,1,0:T(8,128)} async-done(((f32[32,32,128]{2,1,0:T(8,128)}), f32[256,32,128]{2,1,0:T(8,128)}) %all-gather.3.cloned.1.call-update) | async-done | bytes 4194320 | tf_op jit(solution)/shard_map/all_gather | solution.py:139
  483.2 2.7 reduce_sum.19
  489.4 5.8 %all-to-all-start = ((f32[16,1,8192]{2,1,0:T(1,128)}), f32[16,1,8192]{2,1,0:T(1,128)}, u32[]{:S(2)}, u32[]{:S(2)}) async-start(f32[16,1,8192]{2,1,0:T(1,128)} %reshape.256), calls=%async_computation | async-start | bytes 1048576 | tf_op jit(solution)/shard_map/all_to_all | solution.py:141
  499.1 2.7 copy.46
  504.1 4.8 convolution_multiply_fusion
  508.9 3.0 reduce.9
  512.6 2.7 copy.43
  515.3 2.5 reshape.131
  517.8 4.8 fusion.4
  522.6 5.1 convolution_bitcast_fusion
  530.3 6.0 %all-to-all-start.2 = ((f32[16,1,8192]{2,1,0:T(1,128)}), f32[16,1,8192]{2,1,0:T(1,128)S(1)}, u32[]{:S(2)}, u32[]{:S(2)}) async-start(f32[16,1,8192]{2,1,0:T(1,128)} %reshape.258), calls=%async_computation.2 | async-start | bytes 1048576 | tf_op jit(solution)/shard_map/all_to_all | solution.py:145
  536.6 9.5 %all-to-all-done.2 = f32[16,1,8192]{2,1,0:T(1,128)S(1)} async-done(((f32[16,1,8192]{2,1,0:T(1,128)}), f32[16,1,8192]{2,1,0:T(1,128)S(1)}, u32[]{:S(2)}, u32[]{:S(2)}) %all-to-all-start.2) | async-done | bytes 524320 | tf_op jit(solution)/shard_map/all_to_all | solution.py:145
  (203 shorter events, 108.5 us)
Async XLA Ops:
  6.5 476.6 %all-gather.3.cloned.1.call-start = ((), (), s32[]{:S(2)}) async-start(), calls=%async_computation.3 | async-start | bytes 4718592 | tf_op jit(solution)/shard_map/all_gather | solution.py:139
  7.5 22.4 %collective-permute-start.3 = (f32[2,4,32,128]{3,2,1,0:T(8,128)S(1)}, f32[2,4,32,128]{3,2,1,0:T(8,128)S(1)}, u32[]{:S(2)}, u32[]{:S(2)}) collective-permute-start(f32[2,4,32,128]{3,2,1,0:T(8,128)S(1)} %get-tuple-element.46), channel_id=1, source_target_pairs={{0,1},{1,2},{2,3},{3,4},{4,5},{5,6},{6,7},{7,8},{8,9},{9,10},{10,1... | collective-permute-start | bytes 393224 | tf_op jit(solution)/shard_map/ppermute | solution.py:17
  12.1 21.3 %collective-permute-start.2 = (f32[2,4,32,128]{3,2,1,0:T(8,128)S(1)}, f32[2,4,32,128]{3,2,1,0:T(8,128)}, u32[]{:S(2)}, u32[]{:S(2)}) collective-permute-start(f32[2,4,32,128]{3,2,1,0:T(8,128)S(1)} %get-tuple-element.47), channel_id=1, source_target_pairs={{1,0},{2,1},{3,2},{4,3},{5,4},{6,5},{7,6},{8,7},{9,8},{10,9},{11,1... | collective-permute-start | bytes 393224 | tf_op jit(solution)/shard_map/ppermute | solution.py:20
  15.7 40.3 %collective-permute-start.1 = (f32[2,4,32,128]{3,2,1,0:T(8,128)}, f32[2,4,32,128]{3,2,1,0:T(8,128)S(1)}, u32[]{:S(2)}, u32[]{:S(2)}) collective-permute-start(f32[2,4,32,128]{3,2,1,0:T(8,128)} %get-tuple-element.50), channel_id=1, source_target_pairs={{0,1},{1,2},{2,3},{3,4},{4,5},{5,6},{6,7},{7,8},{8,9},{9,10},{10,1... | collective-permute-start | bytes 393224 | tf_op jit(solution)/shard_map/ppermute | solution.py:17
  19.4 36.7 %collective-permute-start = (f32[2,4,32,128]{3,2,1,0:T(8,128)}, f32[2,4,32,128]{3,2,1,0:T(8,128)S(1)}, u32[]{:S(2)}, u32[]{:S(2)}) collective-permute-start(f32[2,4,32,128]{3,2,1,0:T(8,128)} %get-tuple-element.51), channel_id=1, source_target_pairs={{1,0},{2,1},{3,2},{4,3},{5,4},{6,5},{7,6},{8,7},{9,8},{10,9},{11,1... | collective-permute-start | bytes 393224 | tf_op jit(solution)/shard_map/ppermute | solution.py:20
  25.8 7.6 %copy-start.19 = (f32[2,32,32,128]{3,2,1,0:T(8,128)S(1)}, f32[2,32,32,128]{3,2,1,0:T(8,128)}, u32[]{:S(2)}) copy-start(f32[2,32,32,128]{3,2,1,0:T(8,128)} %param.18) | copy-start | bytes 3145732
  49.6 9.1 %copy-start.17 = (f32[2,32,32,128]{3,2,1,0:T(8,128)S(1)}, f32[2,32,32,128]{3,2,1,0:T(8,128)}, u32[]{:S(2)}) copy-start(f32[2,32,32,128]{3,2,1,0:T(8,128)} %param.20) | copy-start | bytes 3145732
  49.7 13.3 %copy-start.11 = (f32[1,2,1024,128]{3,2,1,0:T(8,128)}, f32[1,2,1024,128]{3,2,1,0:T(8,128)S(1)}, u32[]{:S(2)}) copy-start(f32[1,2,1024,128]{3,2,1,0:T(8,128)S(1)} %copy.60) | copy-start | bytes 3145732
  49.7 10.9 %collective-permute-start.5 = (f32[2,4,32,128]{3,2,1,0:T(8,128)S(1)}, f32[2,4,32,128]{3,2,1,0:T(8,128)S(1)}, u32[]{:S(2)}, u32[]{:S(2)}) collective-permute-start(f32[2,4,32,128]{3,2,1,0:T(8,128)S(1)} %get-tuple-element.42), channel_id=1, source_target_pairs={{0,1},{1,2},{2,3},{3,4},{4,5},{5,6},{6,7},{7,8},{8,9},{9,10},{10,1... | collective-permute-start | bytes 393224 | tf_op jit(solution)/shard_map/ppermute | solution.py:17
  53.6 9.3 %collective-permute-start.4 = (f32[2,4,32,128]{3,2,1,0:T(8,128)S(1)}, f32[2,4,32,128]{3,2,1,0:T(8,128)S(1)}, u32[]{:S(2)}, u32[]{:S(2)}) collective-permute-start(f32[2,4,32,128]{3,2,1,0:T(8,128)S(1)} %get-tuple-element.43), channel_id=1, source_target_pairs={{1,0},{2,1},{3,2},{4,3},{5,4},{6,5},{7,6},{8,7},{9,8},{10,9},{11,1... | collective-permute-start | bytes 393224 | tf_op jit(solution)/shard_map/ppermute | solution.py:20
  94.1 7.2 %copy-start.18 = (f32[2,32,32,128]{3,2,1,0:T(8,128)S(1)}, f32[2,32,32,128]{3,2,1,0:T(8,128)}, u32[]{:S(2)}) copy-start(f32[2,32,32,128]{3,2,1,0:T(8,128)} %param.20) | copy-start | bytes 3145732
  97.2 22.8 %collective-permute-start.7 = (f32[2,4,32,128]{3,2,1,0:T(8,128)}, f32[2,4,32,128]{3,2,1,0:T(8,128)S(1)}, u32[]{:S(2)}, u32[]{:S(2)}) collective-permute-start(f32[2,4,32,128]{3,2,1,0:T(8,128)} %get-tuple-element.38), channel_id=1, source_target_pairs={{0,1},{1,2},{2,3},{3,4},{4,5},{5,6},{6,7},{7,8},{8,9},{9,10},{10,1... | collective-permute-start | bytes 393224 | tf_op jit(solution)/shard_map/ppermute | solution.py:17
  109.2 10.8 %copy-start.13 = (f32[1,2,1024,128]{3,2,1,0:T(8,128)S(1)}, f32[1,2,1024,128]{3,2,1,0:T(8,128)}, u32[]{:S(2)}) copy-start(f32[1,2,1024,128]{3,2,1,0:T(8,128)} %copy-done.12) | copy-start | bytes 3145732
  117.9 6.3 %collective-permute-start.6 = (f32[2,4,32,128]{3,2,1,0:T(8,128)S(1)}, f32[2,4,32,128]{3,2,1,0:T(8,128)S(1)}, u32[]{:S(2)}, u32[]{:S(2)}) collective-permute-start(f32[2,4,32,128]{3,2,1,0:T(8,128)S(1)} %get-tuple-element.39), channel_id=1, source_target_pairs={{1,0},{2,1},{3,2},{4,3},{5,4},{6,5},{7,6},{8,7},{9,8},{10,9},{11,1... | collective-permute-start | bytes 393224 | tf_op jit(solution)/shard_map/ppermute | solution.py:20
  127.3 10.3 %copy-start.40 = (f32[16]{0:T(128)S(1)}, f32[16]{0:T(128)}, u32[]{:S(2)}) copy-start(f32[16]{0:T(128)} %reshape.175) | copy-start | bytes 196
  135.6 6.9 %copy-start.16 = (f32[2,131072]{1,0:T(2,128)S(1)}, f32[2,131072]{1,0:T(2,128)}, u32[]{:S(2)}) copy-start(f32[2,131072]{1,0:T(2,128)} %scatter_fusion.1) | copy-start | bytes 3145732
  139.1 20.3 %copy-start.20 = (f32[1,2,1024,128]{3,2,1,0:T(8,128)}, f32[1,2,1024,128]{3,2,1,0:T(8,128)S(1)}, u32[]{:S(2)}) copy-start(f32[1,2,1024,128]{3,2,1,0:T(8,128)S(1)} %copy.64) | copy-start | bytes 3145732
  139.2 19.1 %collective-permute-start.9 = (f32[2,4,32,128]{3,2,1,0:T(8,128)S(1)}, f32[2,4,32,128]{3,2,1,0:T(8,128)S(1)}, u32[]{:S(2)}, u32[]{:S(2)}) collective-permute-start(f32[2,4,32,128]{3,2,1,0:T(8,128)S(1)} %get-tuple-element.34), channel_id=1, source_target_pairs={{0,1},{1,2},{2,3},{3,4},{4,5},{5,6},{6,7},{7,8},{8,9},{9,10},{10,1... | collective-permute-start | bytes 393224 | tf_op jit(solution)/shard_map/ppermute | solution.py:17
  155.7 6.3 %collective-permute-start.8 = (f32[2,4,32,128]{3,2,1,0:T(8,128)S(1)}, f32[2,4,32,128]{3,2,1,0:T(8,128)S(1)}, u32[]{:S(2)}, u32[]{:S(2)}) collective-permute-start(f32[2,4,32,128]{3,2,1,0:T(8,128)S(1)} %get-tuple-element.35), channel_id=1, source_target_pairs={{1,0},{2,1},{3,2},{4,3},{5,4},{6,5},{7,6},{8,7},{9,8},{10,9},{11,1... | collective-permute-start | bytes 393224 | tf_op jit(solution)/shard_map/ppermute | solution.py:20
  165.1 10.4 %copy-start.39 = (f32[16]{0:T(128)S(1)}, f32[16]{0:T(128)}, u32[]{:S(2)}) copy-start(f32[16]{0:T(128)} %reshape.181) | copy-start | bytes 196
  173.3 8.4 %copy-start.34 = (f32[2,256]{1,0:T(2,128)S(1)}, f32[2,256]{1,0:T(2,128)}, u32[]{:S(2)}) copy-start(f32[2,256]{1,0:T(2,128)} %reshape.239) | copy-start | bytes 6148
  173.4 8.4 %copy-start.35 = (f32[2,1,256]{2,1,0:T(1,128)S(1)}, f32[2,1,256]{2,1,0:T(1,128)}, u32[]{:S(2)}) copy-start(f32[2,1,256]{2,1,0:T(1,128)} %get-tuple-element.52) | copy-start | bytes 6148
  173.4 8.4 %copy-start.36 = (f32[2,1,256]{2,1,0:T(1,128)S(1)}, f32[2,1,256]{2,1,0:T(1,128)}, u32[]{:S(2)}) copy-start(f32[2,1,256]{2,1,0:T(1,128)} %get-tuple-element.53) | copy-start | bytes 6148
  173.4 8.4 %copy-start.37 = (f32[2,1,256]{2,1,0:T(1,128)S(1)}, f32[2,1,256]{2,1,0:T(1,128)}, u32[]{:S(2)}) copy-start(f32[2,1,256]{2,1,0:T(1,128)} %get-tuple-element.55) | copy-start | bytes 6148
  173.4 8.4 %copy-start.38 = (pred[2,256]{1,0:T(4,128)(4,1)S(1)}, pred[2,256]{1,0:T(4,128)(4,1)}, u32[]{:S(2)}) copy-start(pred[2,256]{1,0:T(4,128)(4,1)} %get-tuple-element.11) | copy-start | bytes 1540
  173.4 8.4 %copy-start.21 = (f32[1,2,1024,128]{3,1,2,0:T(2,128)S(1)}, f32[1,2,1024,128]{3,1,2,0:T(2,128)}, u32[]{:S(2)}) copy-start(f32[1,2,1024,128]{3,1,2,0:T(2,128)} %copy.111) | copy-start | bytes 3145732
  206.7 12.5 %copy-start.3 = (f32[1,2,1024,128]{3,2,1,0:T(8,128)}, f32[1,2,1024,128]{3,2,1,0:T(8,128)S(1)}, u32[]{:S(2)}) copy-start(f32[1,2,1024,128]{3,2,1,0:T(8,128)S(1)} %copy.68) | copy-start | bytes 3145732
  206.7 4.4 collective-permute-start.11
  208.6 8.4 %collective-permute-start.10 = (f32[2,4,32,128]{3,2,1,0:T(8,128)S(1)}, f32[2,4,32,128]{3,2,1,0:T(8,128)S(1)}, u32[]{:S(2)}, u32[]{:S(2)}) collective-permute-start(f32[2,4,32,128]{3,2,1,0:T(8,128)S(1)} %get-tuple-element.31), channel_id=1, source_target_pairs={{1,0},{2,1},{3,2},{4,3},{5,4},{6,5},{7,6},{8,7},{9,8},{10,9},{11,1... | collective-permute-start | bytes 393224 | tf_op jit(solution)/shard_map/ppermute | solution.py:20
  211.1 8.1 %copy-start = (f32[32,32,128]{2,1,0:T(8,128)S(1)}, f32[32,32,128]{2,1,0:T(8,128)}, u32[]{:S(2)}) copy-start(f32[32,32,128]{2,1,0:T(8,128)} %multiply_multiply_fusion) | copy-start | bytes 1572868
  253.8 15.8 %copy-start.6 = (f32[1,2,1024,128]{3,2,1,0:T(8,128)}, f32[1,2,1024,128]{3,2,1,0:T(8,128)S(1)}, u32[]{:S(2)}) copy-start(f32[1,2,1024,128]{3,2,1,0:T(8,128)S(1)} %copy.71) | copy-start | bytes 3145732
  253.9 4.8 collective-permute-start.13
  255.8 12.4 %collective-permute-start.12 = (f32[2,4,32,128]{3,2,1,0:T(8,128)S(1)}, f32[2,4,32,128]{3,2,1,0:T(8,128)S(1)}, u32[]{:S(2)}, u32[]{:S(2)}) collective-permute-start(f32[2,4,32,128]{3,2,1,0:T(8,128)S(1)} %get-tuple-element.27), channel_id=1, source_target_pairs={{1,0},{2,1},{3,2},{4,3},{5,4},{6,5},{7,6},{8,7},{9,8},{10,9},{11,1... | collective-permute-start | bytes 393224 | tf_op jit(solution)/shard_map/ppermute | solution.py:20
  258.7 11.6 %copy-start.1 = (f32[32,32,128]{2,1,0:T(8,128)S(1)}, f32[32,32,128]{2,1,0:T(8,128)}, u32[]{:S(2)}) copy-start(f32[32,32,128]{2,1,0:T(8,128)} %multiply_multiply_fusion) | copy-start | bytes 1572868
  258.7 11.6 %copy-start.4 = (f32[1,2,1024,128]{3,2,1,0:T(8,128)S(1)}, f32[1,2,1024,128]{3,2,1,0:T(8,128)}, u32[]{:S(2)}) copy-start(f32[1,2,1024,128]{3,2,1,0:T(8,128)} %copy-done.3) | copy-start | bytes 3145732
  280.1 26.9 %copy-start.33 = (f32[1,2,2,128]{3,2,1,0:T(2,128)S(1)}, f32[1,2,2,128]{3,2,1,0:T(2,128)}, u32[]{:S(2)}) copy-start(f32[1,2,2,128]{3,2,1,0:T(2,128)} %get-tuple-element.10) | copy-start | bytes 6148
  305.0 11.9 %copy-start.9 = (f32[1,2,1024,128]{3,2,1,0:T(8,128)}, f32[1,2,1024,128]{3,2,1,0:T(8,128)S(1)}, u32[]{:S(2)}) copy-start(f32[1,2,1024,128]{3,2,1,0:T(8,128)S(1)} %copy.74) | copy-start | bytes 3145732
  305.0 4.4 collective-permute-start.15
  307.1 8.3 %collective-permute-start.14 = (f32[2,4,32,128]{3,2,1,0:T(8,128)S(1)}, f32[2,4,32,128]{3,2,1,0:T(8,128)S(1)}, u32[]{:S(2)}, u32[]{:S(2)}) collective-permute-start(f32[2,4,32,128]{3,2,1,0:T(8,128)S(1)} %get-tuple-element.23), channel_id=1, source_target_pairs={{1,0},{2,1},{3,2},{4,3},{5,4},{6,5},{7,6},{8,7},{9,8},{10,9},{11,1... | collective-permute-start | bytes 393224 | tf_op jit(solution)/shard_map/ppermute | solution.py:20
  309.4 8.1 %copy-start.2 = (f32[32,32,128]{2,1,0:T(8,128)S(1)}, f32[32,32,128]{2,1,0:T(8,128)}, u32[]{:S(2)}) copy-start(f32[32,32,128]{2,1,0:T(8,128)} %multiply_multiply_fusion) | copy-start | bytes 1572868
  309.4 8.1 %copy-start.7 = (f32[1,2,1024,128]{3,2,1,0:T(8,128)S(1)}, f32[1,2,1024,128]{3,2,1,0:T(8,128)}, u32[]{:S(2)}) copy-start(f32[1,2,1024,128]{3,2,1,0:T(8,128)} %copy-done.6) | copy-start | bytes 3145732
  328.4 71.5 %copy-start.5 = (f32[1,2,1024,128]{3,2,1,0:T(8,128)S(1)}, f32[1,2,1024,128]{3,2,1,0:T(8,128)}, u32[]{:S(2)}) copy-start(f32[1,2,1024,128]{3,2,1,0:T(8,128)} %copy-done.3) | copy-start | bytes 3145732
  328.4 71.5 %copy-start.8 = (f32[1,2,1024,128]{3,2,1,0:T(8,128)S(1)}, f32[1,2,1024,128]{3,2,1,0:T(8,128)}, u32[]{:S(2)}) copy-start(f32[1,2,1024,128]{3,2,1,0:T(8,128)} %copy-done.6) | copy-start | bytes 3145732
  328.4 71.5 %copy-start.10 = (f32[1,2,1024,128]{3,2,1,0:T(8,128)S(1)}, f32[1,2,1024,128]{3,2,1,0:T(8,128)}, u32[]{:S(2)}) copy-start(f32[1,2,1024,128]{3,2,1,0:T(8,128)} %copy-done.9) | copy-start | bytes 3145732
  408.9 80.6 %all-to-all-start.1 = ((f32[16,1,8192]{2,1,0:T(1,128)}), f32[16,1,8192]{2,1,0:T(1,128)S(1)}, u32[]{:S(2)}, u32[]{:S(2)}) async-start(f32[16,1,8192]{2,1,0:T(1,128)} %reshape.254), calls=%async_computation.1 | async-start | bytes 1048576 | tf_op jit(solution)/shard_map/all_to_all | solution.py:142
  489.4 19.5 %all-to-all-start = ((f32[16,1,8192]{2,1,0:T(1,128)}), f32[16,1,8192]{2,1,0:T(1,128)}, u32[]{:S(2)}, u32[]{:S(2)}) async-start(f32[16,1,8192]{2,1,0:T(1,128)} %reshape.256), calls=%async_computation | async-start | bytes 1048576 | tf_op jit(solution)/shard_map/all_to_all | solution.py:141
  527.7 8.5 %copy-start.30 = (f32[32,32,128]{2,1,0:T(8,128)S(1)}, f32[32,32,128]{2,1,0:T(8,128)}, u32[]{:S(2)}) copy-start(f32[32,32,128]{2,1,0:T(8,128)} %param.14) | copy-start | bytes 1572868
  530.3 15.9 %all-to-all-start.2 = ((f32[16,1,8192]{2,1,0:T(1,128)}), f32[16,1,8192]{2,1,0:T(1,128)S(1)}, u32[]{:S(2)}, u32[]{:S(2)}) async-start(f32[16,1,8192]{2,1,0:T(1,128)} %reshape.258), calls=%async_computation.2 | async-start | bytes 1048576 | tf_op jit(solution)/shard_map/all_to_all | solution.py:145
  (13 other events, 34.1 us)
Sparse Core Ops, SparseCore 0:
  404.4 78.7 all-gather.2
